TPU v7x, 512 devices: a whole 4x8x8 slice. The times are simulated.
512 devices in a mesh: ctx: 64 (over z, y_lo, core), fsdp: 8 (over y_hi, x).
Axes of the slice: x: 4, y: 8 (y_hi: 2, y_lo: 4; y = y_hi * 4 + y_lo), z: 8, core: 2. Of those that a mesh axis runs over, the one named last changes fastest.
Arguments:
- tokens: bfloat16 [8192, 4096], P('ctx', 'fsdp'), may hold values from -130 to 130, as said below
- w_query: bfloat16 [4096, 4096], P('ctx', 'fsdp'), may hold values from -0.09375 to 0.09375
- key_matrix: bfloat16 [4096, 1024], P('ctx', 'fsdp'), may hold values from -0.09375 to 0.09375
- value_matrix: bfloat16 [4096, 1024], P('ctx', 'fsdp'), may hold values from -0.09375 to 0.09375
- w_out: bfloat16 [4096, 4096], P('fsdp', 'ctx'), may hold values from -0.75 to 0.75
Outputs:
- mixed: bfloat16 [8192, 4096], P('ctx', 'fsdp')
Inputs may be any that keep to these rules, and one draw needn't show every extreme that they name: `tokens`: no structure of the entries is promised.
All inputs are finite; a program needn't handle non-finite values.
Results may differ from a plain program's by a relative error of at most 0.014.
The roundings to bfloat16 on the way count: a program that leaves them out, or rounds other values in their place, can miss the bound.
Values may be sent and summed in bfloat16 or wider, within the bound.
A program may use at most 64 MiB of HBM per device.

v0:
```python
import math
import jax
import jax.numpy as jnp
from jax import lax
from jax.sharding import PartitionSpec as P

HEAD_SIZE = 128


def rotate_heads(values, positions):
    tok_count = values.shape[0]
    head_count = values.shape[1] // HEAD_SIZE
    half_dim = HEAD_SIZE // 2
    inverse_freq = jnp.power(
        jnp.float32(500000.0), -jnp.arange(half_dim, dtype=jnp.float32) * 2.0 / HEAD_SIZE
    )
    angles = positions.astype(jnp.float32)[:, None] * inverse_freq[None, :]
    cosine = jnp.cos(angles)[:, None, :]
    sine_table = jnp.sin(angles)[:, None, :]
    shaped = values.reshape(tok_count, head_count, HEAD_SIZE)
    first_half = shaped[:, :, :half_dim]
    second = shaped[:, :, half_dim:]
    turned = jnp.concatenate(
        [first_half * cosine - second * sine_table, second * cosine + first_half * sine_table],
        axis=2,
    )
    return turned.reshape(tok_count, head_count * HEAD_SIZE).astype(jnp.bfloat16)


def body(tokens, w_query, key_matrix, value_matrix, w_out):
    features = lax.all_gather(tokens, "fsdp", axis=1, tiled=True)
    tok_count = features.shape[0]
    positions = lax.axis_index("ctx") * tok_count + jnp.arange(tok_count, dtype=jnp.int32)

    def add_rows(weight_piece):
        return jnp.dot(features, weight_piece, preferred_element_type=jnp.float32)

    query_sum = add_rows(lax.all_gather(w_query, "ctx", axis=0, tiled=True))
    key_sum = add_rows(lax.all_gather(key_matrix, "ctx", axis=0, tiled=True))
    value_sum = add_rows(lax.all_gather(value_matrix, "ctx", axis=0, tiled=True))
    queries = rotate_heads(query_sum, positions)
    projected_keys = rotate_heads(key_sum, positions)
    projected_values = value_sum.astype(jnp.bfloat16)
    kv_heads = projected_keys.shape[1] // HEAD_SIZE
    queries_per_group = queries.shape[1] // projected_keys.shape[1]
    stacked = (
        queries.reshape(tok_count, kv_heads, queries_per_group, HEAD_SIZE)
        .transpose(1, 2, 0, 3)
        .reshape(kv_heads, queries_per_group * tok_count, HEAD_SIZE)
    )
    query_pos = jnp.tile(positions, queries_per_group)
    score_scale = 1.0 / math.sqrt(HEAD_SIZE)

    def update(attn_state, key_block, value_block, key_start):
        row_max, row_total, accum = attn_state
        block_rows = key_block.shape[0]
        key_heads = key_block.reshape(block_rows, kv_heads, HEAD_SIZE)
        value_heads = value_block.reshape(block_rows, kv_heads, HEAD_SIZE)
        scores = (
            jnp.einsum("gqd,kgd->gqk", stacked, key_heads, preferred_element_type=jnp.float32)
            * score_scale
        )
        key_pos = key_start + jnp.arange(block_rows, dtype=jnp.int32)
        allowed = (key_pos[None, :] <= query_pos[:, None])[None]
        masked = jnp.where(allowed, scores, jnp.float32(-1e30))
        new_max = jnp.maximum(row_max, jnp.max(masked, axis=2))
        exp_weights = jnp.where(allowed, jnp.exp(masked - new_max[:, :, None]), jnp.float32(0.0))
        factor = jnp.exp(row_max - new_max)
        row_total = row_total * factor + jnp.sum(exp_weights, axis=2)
        accum = accum * factor[:, :, None] + jnp.einsum(
            "gqk,kgd->gqd",
            exp_weights.astype(jnp.bfloat16),
            value_heads,
            preferred_element_type=jnp.float32,
        )
        return (new_max, row_total, accum)

    query_rows = queries_per_group * tok_count
    initial = (
        jnp.full((kv_heads, query_rows), -1e30, jnp.float32),
        jnp.zeros((kv_heads, query_rows), jnp.float32),
        jnp.zeros((kv_heads, query_rows, HEAD_SIZE), jnp.float32),
    )
    key_piece = lax.all_gather(projected_keys, "ctx", axis=0, tiled=True)
    value_piece = lax.all_gather(projected_values, "ctx", axis=0, tiled=True)
    block_rows = min(tok_count, key_piece.shape[0])
    block_count = key_piece.shape[0] // block_rows

    def advance(block_index, carried):
        key_start = block_index * block_rows
        key_block = lax.dynamic_slice_in_dim(key_piece, block_index * block_rows, block_rows, 0)
        value_block = lax.dynamic_slice_in_dim(value_piece, block_index * block_rows, block_rows, 0)
        return update(carried, key_block, value_block, key_start)

    row_max, row_total, accum = lax.fori_loop(0, block_count, advance, initial)
    normed = accum / row_total[:, :, None]
    attn_out = (
        normed.reshape(kv_heads, queries_per_group, tok_count, HEAD_SIZE)
        .transpose(2, 0, 1, 3)
        .reshape(tok_count, kv_heads * queries_per_group * HEAD_SIZE)
        .astype(jnp.bfloat16)
    )
    partial_out = jnp.dot(
        attn_out,
        lax.all_gather(w_out, "ctx", axis=1, tiled=True),
        preferred_element_type=jnp.float32,
    )
    return lax.psum_scatter(
        partial_out.astype(jnp.bfloat16), "fsdp", scatter_dimension=1, tiled=True
    )


def solution(mesh):
    in_specs = (
        P("ctx", "fsdp"),
        P("ctx", "fsdp"),
        P("ctx", "fsdp"),
        P("ctx", "fsdp"),
        P("fsdp", "ctx"),
    )
    out_specs = P("ctx", "fsdp")
    return jax.shard_map(body, mesh=mesh, in_specs=in_specs, out_specs=out_specs, check_vma=False)
```

profile of v0, /device:TPU:2, one launch (start us, length us, event | category | flops | bytes accessed | tf_op | source)
XLA Modules:
  0.0 912.1 jit_solution(4390556370071659170)
XLA Ops:
  9.4 69.6 %all-gather.9.cloned.1.call-done = bf16[128,4096]{1,0:T(8,128)(2,1)} async-done(((bf16[128,512]{1,0:T(8,128)(2,1)}), bf16[128,4096]{1,0:T(8,128)(2,1)}) %all-gather.9.cloned.1.call-update) | async-done | bytes 1048592 | tf_op jit(solution)/shard_map/all_gather | solution.py:31
  79.0 117.3 %all-gather.11.cloned.1.call-done = bf16[4096,128]{1,0:T(8,128)(2,1)} async-done(((bf16[64,128]{1,0:T(8,128)(2,1)}), bf16[4096,128]{1,0:T(8,128)(2,1)}) %all-gather.11.cloned.1.call-update) | async-done | bytes 1048592 | tf_op jit(solution)/shard_map/all_gather | solution.py:39
  196.3 2.1 convolution_bitcast_fusion.1
  199.3 114.5 %all-gather.15.cloned.1.call-done = bf16[4096,128]{1,0:T(8,128)(2,1)} async-done(((bf16[64,128]{1,0:T(8,128)(2,1)}), bf16[4096,128]{1,0:T(8,128)(2,1)}) %all-gather.15.cloned.1.call-update) | async-done | bytes 1048592 | tf_op jit(solution)/shard_map/all_gather | solution.py:40
  313.7 2.6 convolution_convert_fusion.1
  317.5 116.0 %all-gather.13.cloned.1.call-done = bf16[4096,512]{1,0:T(8,128)(2,1)} async-done(((bf16[64,512]{1,0:T(8,128)(2,1)}), bf16[4096,512]{1,0:T(8,128)(2,1)}) %all-gather.13.cloned.1.call-update) | async-done | bytes 4194320 | tf_op jit(solution)/shard_map/all_gather | solution.py:38
  433.4 2.9 fusion.33
  437.0 111.6 %all-gather.21.cloned.1.call-done = bf16[8192,1,128]{0,2,1:T(8,128)(2,1)} async-done(((bf16[128,1,128]{0,2,1:T(8,128)(2,1)}), bf16[8192,1,128]{0,2,1:T(8,128)(2,1)}) %all-gather.21.cloned.1.call-update) | async-done | bytes 2097168 | tf_op jit(solution)/shard_map/all_gather | solution.py:84
  548.6 116.5 %all-gather.17.cloned.1.call-done = bf16[8192,128]{1,0:T(8,128)(2,1)} async-done(((bf16[128,128]{1,0:T(8,128)(2,1)}), bf16[8192,128]{1,0:T(8,128)(2,1)}) %all-gather.17.cloned.1.call-update) | async-done | bytes 2097168 | tf_op jit(solution)/shard_map/all_gather | solution.py:85
  665.1 145.2 %while.18 = (s32[]{:T(128)}, f32[1,512]{1,0:T(1,128)S(1)}, f32[1,512]{1,0:T(1,128)S(1)}, f32[1,512,128]{2,1,0:T(8,128)S(1)}, bf16[8192,128]{0,1:T(8,128)(2,1)}, ...) while((s32[]{:T(128)}, f32[1,512]{1,0:T(1,128)S(1)}, ...), condition=%wide.region_3.4_spmd.clone, body=%wide.region_0.3_spmd.clone.sunk | while | flops 34540164 | bytes 1551035 | solution.py:95
  666.2 1.1 fusion.55
  670.8 1.1 fusion.55
  675.3 1.1 fusion.55
  679.8 1.1 fusion.55
  684.4 1.1 fusion.55
  688.9 1.1 fusion.55
  691.2 1.1 fusion.55
  695.7 1.1 fusion.55
  700.3 1.1 fusion.55
  704.8 1.1 fusion.55
  709.4 1.1 fusion.55
  711.6 1.1 fusion.55
  713.9 1.1 fusion.55
  716.2 1.1 fusion.55
  718.4 1.1 fusion.55
  732.1 1.1 fusion.55
  754.8 1.1 fusion.55
  768.4 1.1 fusion.55
  791.1 1.1 fusion.55
  804.7 1.1 fusion.55
  810.6 4.7 convolution_convert_fusion
  815.3 89.9 %reduce-scatter.2.cloned.1.call-done = bf16[128,512]{1,0:T(8,128)(2,1)} async-done(((bf16[128,4096]{1,0:T(8,128)(2,1)}), bf16[128,512]{1,0:T(8,128)(2,1)}) %reduce-scatter.2.cloned.1.call-update) | async-done | bytes 131088 | tf_op jit(solution)/shard_map/reduce_scatter | solution.py:108
  (526 shorter events, 125.0 us)
Async XLA Ops:
  6.5 72.4 %all-gather.9.cloned.1.call-start = ((), (), s32[]{:S(2)}) async-start(), calls=%async_computation.1 | async-start | bytes 1179648 | tf_op jit(solution)/shard_map/all_gather | solution.py:31
  7.3 189.0 %all-gather.11.cloned.1.call-start = ((), (), s32[]{:S(2)}) async-start(), calls=%async_computation.2 | async-start | bytes 1064960 | tf_op jit(solution)/shard_map/all_gather | solution.py:39
  8.0 305.7 %all-gather.15.cloned.1.call-start = ((), (), s32[]{:S(2)}) async-start(), calls=%async_computation.4 | async-start | bytes 1064960 | tf_op jit(solution)/shard_map/all_gather | solution.py:40
  8.7 424.7 %all-gather.13.cloned.1.call-start = ((), (), s32[]{:S(2)}) async-start(), calls=%async_computation.3 | async-start | bytes 4259840 | tf_op jit(solution)/shard_map/all_gather | solution.py:38
  9.3 539.2 %all-gather.21.cloned.1.call-start = ((), (), s32[]{:S(2)}) async-start(), calls=%async_computation.8 | async-start | bytes 2129920 | tf_op jit(solution)/shard_map/all_gather | solution.py:84
  79.0 354.5 %copy-start = (bf16[128,4096]{1,0:T(8,128)(2,1)S(1)}, bf16[128,4096]{1,0:T(8,128)(2,1)}, u32[]{:S(2)}) copy-start(bf16[128,4096]{1,0:T(8,128)(2,1)} %all-gather.9.cloned.1.call-done) | copy-start | bytes 3145732
  199.2 465.9 %all-gather.17.cloned.1.call-start = ((), (), s32[]{:S(2)}) async-start(), calls=%async_computation.5 | async-start | bytes 2129920 | tf_op jit(solution)/shard_map/all_gather | solution.py:85
  316.3 494.3 %all-gather.19.cloned.1.call-start = ((), (), s32[]{:S(2)}) async-start(), calls=%async_computation.6 | async-start | bytes 4259840 | tf_op jit(solution)/shard_map/all_gather | solution.py:105
  317.1 588.2 %reduce-scatter.2.cloned.1.call-start = ((), (), s32[]{:S(2)}) async-start(), calls=%async_computation.7 | async-start | bytes 1179648 | tf_op jit(solution)/shard_map/reduce_scatter | solution.py:108
Sparse Core Ops, SparseCore 0:
  10.4 68.5 all-gather.8
  81.1 115.1 all-gather.10
  198.5 115.2 all-gather.14
  315.7 117.6 all-gather.12
  435.3 113.1 all-gather.20
  550.6 114.4 all-gather.16
  667.2 117.7 all-gather.18
  815.5 89.7 reduce-scatter.1
where the time goes:
time: 921 us; the launch traced here: 912 us
  waiting for transfers between devices  739 us (80%)
  matrix products  144 us (16%)
  between operations  13.6 us (1%)
  other arithmetic  10.8 us (1%)
    all_gather x1, waiting for transfers between devices, body(): key_sum = add_rows(lax.all_gather(key_matrix, 'ctx', axis=0, tiled=True))  117 us
    all_gather x1, waiting for transfers between devices, body(): value_piece = lax.all_gather(projected_values, 'ctx', axis=0, tiled=True)  117 us
    all_gather x1, waiting for transfers between devices, body(): query_sum = add_rows(lax.all_gather(w_query, 'ctx', axis=0, tiled=True))  116 us
    all_gather x1, waiting for transfers between devices, body(): lax.all_gather(value_matrix, 'ctx', axis=0, tiled=True)  114 us
    all_gather x1, waiting for transfers between devices, body(): key_piece = lax.all_gather(projected_keys, 'ctx', axis=0, tiled=True)  112 us
    reduce_scatter x1, waiting for transfers between devices, body(): lax.psum_scatter(partial_out.astype(jnp.bfloat16), 'fsdp', scatter_dimens...  89.9 us
    all_gather x1, waiting for transfers between devices, body(): features = lax.all_gather(tokens, 'fsdp', axis=1, tiled=True)  69.6 us
    dot_general x64, matrix products, update(): jnp.einsum('gqk,kgd->gqd', exp_weights.astype(jnp.bfloat16), value_heads,...  68.1 us
  transfers between devices with their start and end apart: 8, of which 7 were waited for; matrix products, arithmetic and copies ran while one was open for 16% of the time, Pallas kernels for 0%

commit v1 on v0

--- a/solution.py
+++ b/solution.py
@@ -82,7 +82,8 @@
         jnp.zeros((kv_heads, query_rows, HEAD_SIZE), jnp.float32),
     )
     key_piece = lax.all_gather(projected_keys, "ctx", axis=0, tiled=True)
-    value_piece = lax.all_gather(projected_values, "ctx", axis=0, tiled=True)
+    repeated = jnp.stack([projected_values] * lax.axis_size("ctx"))
+    value_piece = jnp.concatenate(lax.all_to_all(repeated, "ctx", 0, 0), axis=0)
     block_rows = min(tok_count, key_piece.shape[0])
     block_count = key_piece.shape[0] // block_rows
 

time: 921 us -> 804 us (0.87)
  waiting for transfers between devices: 739 us -> 663 us
  matrix products: 144 us -> 95.3 us
    all_gather x1 -> x0, waiting for transfers between devices: 117 us -> none  [body(): value_piece = lax.all_gather(projected_values, 'ctx', axis=0, tiled=True)]
    dot_general x64, matrix products: 68.1 us -> 19.6 us  [update(): jnp.einsum('gqk,kgd->gqd', exp_weights.astype(jnp.bfloat16), value_heads,...]
    all_gather x1, waiting for transfers between devices: 0.02 us -> 21 us  [body(): lax.all_gather(w_out, 'ctx', axis=1, tiled=True)]
    all_gather x1, waiting for transfers between devices: 116 us -> 136 us  [body(): query_sum = add_rows(lax.all_gather(w_query, 'ctx', axis=0, tiled=True))]
  transfers between devices with their start and end apart: 8 -> 8, of which waited for: 7 -> 7; matrix products, arithmetic and copies ran while one was open for 16% -> 13% of each run, Pallas kernels for 0% -> 0%
where the time goes in v1:
time: 804 us; the launch traced here: 799 us
  waiting for transfers between devices  663 us (82%)
  matrix products  95.3 us (12%)
  between operations  13.6 us (2%)
  other arithmetic  11.4 us (1%)
    all_gather x1, waiting for transfers between devices, body(): query_sum = add_rows(lax.all_gather(w_query, 'ctx', axis=0, tiled=True))  136 us
    all_gather x1, waiting for transfers between devices, body(): key_sum = add_rows(lax.all_gather(key_matrix, 'ctx', axis=0, tiled=True))  117 us
    all_gather x1, waiting for transfers between devices, body(): lax.all_gather(value_matrix, 'ctx', axis=0, tiled=True)  115 us
    all_gather x1, waiting for transfers between devices, body(): key_piece = lax.all_gather(projected_keys, 'ctx', axis=0, tiled=True)  111 us
    reduce_scatter x1, waiting for transfers between devices, body(): lax.psum_scatter(partial_out.astype(jnp.bfloat16), 'fsdp', scatter_dimens...  90.5 us
    all_gather x1, waiting for transfers between devices, body(): features = lax.all_gather(tokens, 'fsdp', axis=1, tiled=True)  69.6 us
    dot_general x64, matrix products, update(): jnp.einsum('gqd,kgd->gqk', stacked, key_heads, preferred_element_type=jnp...  63.3 us
    all_gather x1, waiting for transfers between devices, body(): lax.all_gather(w_out, 'ctx', axis=1, tiled=True)  21 us
  transfers between devices with their start and end apart: 8, of which 7 were waited for; matrix products, arithmetic and copies ran while one was open for 13% of the time, Pallas kernels for 0%

profile of v1, /device:TPU:2, one launch (start us, length us, event | category | flops | bytes accessed | tf_op | source)
XLA Modules:
  0.0 799.0 jit_solution(15346242149463028472)
XLA Ops:
  9.4 69.6 %all-gather.8.cloned.1.call-done = bf16[128,4096]{1,0:T(8,128)(2,1)} async-done(((bf16[128,512]{1,0:T(8,128)(2,1)}), bf16[128,4096]{1,0:T(8,128)(2,1)}) %all-gather.8.cloned.1.call-update) | async-done | bytes 1048592 | tf_op jit(solution)/shard_map/all_gather | solution.py:31
  79.0 117.3 %all-gather.10.cloned.1.call-done = bf16[4096,128]{1,0:T(8,128)(2,1)} async-done(((bf16[64,128]{1,0:T(8,128)(2,1)}), bf16[4096,128]{1,0:T(8,128)(2,1)}) %all-gather.10.cloned.1.call-update) | async-done | bytes 1048592 | tf_op jit(solution)/shard_map/all_gather | solution.py:39
  196.3 2.1 convolution_bitcast_fusion.1
  199.2 114.5 %all-gather.14.cloned.1.call-done = bf16[4096,128]{1,0:T(8,128)(2,1)} async-done(((bf16[64,128]{1,0:T(8,128)(2,1)}), bf16[4096,128]{1,0:T(8,128)(2,1)}) %all-gather.14.cloned.1.call-update) | async-done | bytes 1048592 | tf_op jit(solution)/shard_map/all_gather | solution.py:40
  313.7 2.0 convolution_convert_fusion.1
  315.7 1.8 stack.2
  317.5 7.4 all-to-all-start
  326.6 136.4 %all-gather.12.cloned.1.call-done = bf16[4096,512]{1,0:T(8,128)(2,1)} async-done(((bf16[64,512]{1,0:T(8,128)(2,1)}), bf16[4096,512]{1,0:T(8,128)(2,1)}) %all-gather.12.cloned.1.call-update) | async-done | bytes 4194320 | tf_op jit(solution)/shard_map/all_gather | solution.py:38
  463.0 3.6 fusion.33
  466.7 1.0 reshape.206
  468.2 110.6 %all-gather.18.cloned.1.call-done = bf16[8192,1,128]{0,2,1:T(8,128)(2,1)} async-done(((bf16[128,1,128]{0,2,1:T(8,128)(2,1)}), bf16[8192,1,128]{0,2,1:T(8,128)(2,1)}) %all-gather.18.cloned.1.call-update) | async-done | bytes 2097168 | tf_op jit(solution)/shard_map/all_gather | solution.py:84
  578.8 96.8 %while.18 = (s32[]{:T(128)}, f32[1,512]{1,0:T(1,128)S(1)}, f32[1,512]{1,0:T(1,128)S(1)}, f32[1,512,128]{2,1,0:T(8,128)S(1)}, bf16[8192,128]{0,1:T(8,128)(2,1)}, ...) while((s32[]{:T(128)}, f32[1,512]{1,0:T(1,128)S(1)}, ...), condition=%wide.region_3.4_spmd.clone, body=%wide.region_0.3_spmd.clone.sunk | while | flops 34540164 | bytes 1551035 | solution.py:96
  584.8 1.0 fusion.51
  587.9 1.0 fusion.51
  590.9 1.0 fusion.51
  595.4 1.0 fusion.51
  601.5 1.0 fusion.51
  603.0 1.0 fusion.51
  604.5 1.0 fusion.51
  610.6 1.0 fusion.51
  615.1 1.0 fusion.51
  616.6 1.0 fusion.51
  621.2 1.0 fusion.51
  624.2 1.0 fusion.51
  634.8 1.0 fusion.51
  637.8 1.0 fusion.51
  643.9 1.0 fusion.51
  648.4 1.0 fusion.51
  651.4 1.0 fusion.51
  675.9 21.0 %all-gather.16.cloned.1.call-done = bf16[512,4096]{0,1:T(8,128)(2,1)} async-done(((bf16[512,64]{0,1:T(8,128)(2,1)}), bf16[512,4096]{0,1:T(8,128)(2,1)}) %all-gather.16.cloned.1.call-update) | async-done | bytes 4194320 | tf_op jit(solution)/shard_map/all_gather | solution.py:106
  696.9 4.7 convolution_convert_fusion
  701.6 90.5 %reduce-scatter.2.cloned.1.call-done = bf16[128,512]{1,0:T(8,128)(2,1)} async-done(((bf16[128,4096]{1,0:T(8,128)(2,1)}), bf16[128,512]{1,0:T(8,128)(2,1)}) %reduce-scatter.2.cloned.1.call-update) | async-done | bytes 131088 | tf_op jit(solution)/shard_map/reduce_scatter | solution.py:109
  (528 shorter events, 81.4 us)
Async XLA Ops:
  6.5 72.4 %all-gather.8.cloned.1.call-start = ((), (), s32[]{:S(2)}) async-start(), calls=%async_computation.2 | async-start | bytes 1179648 | tf_op jit(solution)/shard_map/all_gather | solution.py:31
  7.3 189.0 %all-gather.10.cloned.1.call-start = ((), (), s32[]{:S(2)}) async-start(), calls=%async_computation.3 | async-start | bytes 1064960 | tf_op jit(solution)/shard_map/all_gather | solution.py:39
  8.0 305.7 %all-gather.14.cloned.1.call-start = ((), (), s32[]{:S(2)}) async-start(), calls=%async_computation.5 | async-start | bytes 1064960 | tf_op jit(solution)/shard_map/all_gather | solution.py:40
  8.7 454.3 %all-gather.12.cloned.1.call-start = ((), (), s32[]{:S(2)}) async-start(), calls=%async_computation.4 | async-start | bytes 4259840 | tf_op jit(solution)/shard_map/all_gather | solution.py:38
  9.3 569.5 %all-gather.18.cloned.1.call-start = ((), (), s32[]{:S(2)}) async-start(), calls=%async_computation.8 | async-start | bytes 2129920 | tf_op jit(solution)/shard_map/all_gather | solution.py:84
  9.4 308.1 %copy-start.1 = (f32[128]{0:T(128)}, f32[128]{0:T(128)S(1)}, u32[]{:S(2)}) copy-start(f32[128]{0:T(128)S(1)} %fusion.31) | copy-start | bytes 1540
  199.2 263.8 %copy-start = (bf16[128,4096]{1,0:T(8,128)(2,1)S(1)}, bf16[128,4096]{1,0:T(8,128)(2,1)}, u32[]{:S(2)}) copy-start(bf16[128,4096]{1,0:T(8,128)(2,1)} %all-gather.8.cloned.1.call-done) | copy-start | bytes 3145732
  317.5 261.2 %all-to-all-start = ((bf16[64,128,128]{2,1,0:T(8,128)(2,1)}), bf16[64,128,128]{2,1,0:T(8,128)(2,1)S(1)}, u32[]{:S(2)}, u32[]{:S(2)}) async-start(bf16[64,128,128]{2,1,0:T(8,128)(2,1)} %stack.2), calls=%async_computation | async-start | bytes 4194304 | tf_op jit(solution)/shard_map/all_to_all | solution.py:86
  324.9 372.0 %all-gather.16.cloned.1.call-start = ((), (), s32[]{:S(2)}) async-start(), calls=%async_computation.6 | async-start | bytes 4259840 | tf_op jit(solution)/shard_map/all_gather | solution.py:106
  325.5 466.6 %reduce-scatter.2.cloned.1.call-start = ((), (), s32[]{:S(2)}) async-start(), calls=%async_computation.7 | async-start | bytes 1179648 | tf_op jit(solution)/shard_map/reduce_scatter | solution.py:109
Sparse Core Ops, SparseCore 0:
  10.4 68.5 all-gather.7
  81.1 115.1 all-gather.9
  198.5 115.2 all-gather.13
  315.7 147.2 all-gather.11
  464.9 113.8 all-gather.17
  580.8 116.0 all-gather.15
  701.7 90.3 reduce-scatter.1
